TPU v7x, 32 devices: a whole 2x2x4 slice. The times are simulated.
32 devices in a mesh: lat: 8 (over z, y), lon: 4 (over x, core).
Axes of the slice: x: 2, y: 2, z: 4, core: 2. Of those that a mesh axis runs over, the one named last changes fastest.
Arguments:
- grid_field: float32 [384, 64, 512], P(None, 'lat', 'lon'), may hold values from -6 to 6
- disco_dlat: int32 [64, 16], P('lat'), may hold values from -2 to 2
- disco_dlon: int32 [64, 16], P('lat'), may hold values from -2 to 2
- disco_basis: int32 [64, 16], P('lat'), may hold values from 0 to 3
- disco_quad: float32 [64, 16], P('lat'), may hold values from 0.05 to 0.5
- disco_weight: bfloat16 [4, 384, 384], replicated, may hold values from -0.3125 to 0.3125
- norm_gain: float32 [384], replicated, may hold values from 0.1 to 1.9
- spectral_filter: float32 [384, 64], replicated, may hold values from -6 to 6
- mix_weight: bfloat16 [384, 384], replicated, may hold values from -0.3125 to 0.3125
Outputs:
- updated: float32 [384, 64, 512], P(None, 'lat', 'lon')
All inputs are finite; a program needn't handle non-finite values.
Results may differ from a plain program's by a relative error of at most 0.0044.
Values may be sent and summed in bfloat16 or wider, within the bound.
A program may use at most 64 MiB of HBM per device.

v0:
```python
import math

import jax
import jax.numpy as jnp
from jax import lax
from jax.sharding import PartitionSpec as P

M_DEV = 8
HALO = 2


def padded_2(cells, sides, width):
    for axis, dim in sides:
        count = lax.axis_size(axis)
        head = lax.slice_in_dim(cells, 0, width, axis=dim)
        tail = lax.slice_in_dim(cells, cells.shape[dim] - width, cells.shape[dim], axis=dim)
        cells = jnp.concatenate(
            [
                lax.ppermute(tail, axis, [(i, (i + 1) % count) for i in range(count)]),
                cells,
                lax.ppermute(head, axis, [((i + 1) % count, i) for i in range(count)]),
            ],
            axis=dim,
        )
    return cells


def legendre_table(first_order, local_orders, all_orders, degrees, nlat):
    lat_pos = jnp.arange(nlat, dtype=jnp.float32)
    colatitude = math.pi * (lat_pos + 0.5) / nlat
    cosine = jnp.cos(colatitude)
    sine = jnp.sin(colatitude)
    counters = jnp.arange(1, all_orders, dtype=jnp.float32)
    cumulative = jnp.concatenate(
        [
            jnp.zeros((1,), jnp.float32),
            jnp.cumsum(jnp.log((2.0 * counters - 1.0) / (2.0 * counters))),
        ]
    )
    log_product = lax.dynamic_slice_in_dim(cumulative, first_order, local_orders)
    orders = first_order + jnp.arange(local_orders, dtype=jnp.int32)
    order_real = orders.astype(jnp.float32)[:, None]
    log_seed = (
        0.5 * (jnp.log((2.0 * order_real + 1.0) / (4.0 * math.pi)) + log_product[:, None])
        + order_real * jnp.log(sine)[None, :]
    )
    rescale = jnp.clip(-log_seed, 0.0, 80.0)
    seed_value = jnp.exp(log_seed + rescale)
    undo = jnp.exp(-rescale)

    def advance(state_pair, degree):
        previous, before_last = state_pair
        degree_real = degree.astype(jnp.float32)
        factor_a = jnp.sqrt(
            jnp.maximum(4.0 * degree_real**2 - 1.0, 1.0)
            / jnp.maximum(degree_real**2 - order_real**2, 1.0)
        )
        factor_b = jnp.sqrt(
            jnp.maximum((degree_real - 1.0) ** 2 - order_real**2, 0.0)
            / jnp.maximum(4.0 * (degree_real - 1.0) ** 2 - 1.0, 1.0)
        )
        recurred = factor_a * (cosine[None, :] * previous - factor_b * before_last)
        current = jnp.where(
            degree == orders[:, None],
            seed_value,
            jnp.where(degree > orders[:, None], recurred, 0.0),
        )
        return ((current, previous), current * undo)

    empty = jnp.zeros((local_orders, nlat), jnp.float32)
    final_pair, table = lax.scan(
        advance, (empty, empty), jnp.arange(degrees, dtype=jnp.int32), unroll=8
    )
    return table


def disco_rows(padded, disco_dlat, disco_dlon, disco_basis, disco_quad, disco_weight, width):
    basis_count = disco_weight.shape[0]
    channels = padded.shape[0]
    zero_index = jnp.zeros((), jnp.int32)

    def one_row(inputs):
        row_index, lat_offsets, lon_offsets, basis_row, quad_row = inputs
        sources = row_index + HALO + lat_offsets
        begins = HALO + lon_offsets

        def take(source, begin):
            return lax.dynamic_slice(padded, (zero_index, source, begin), (channels, 1, width))[
                :, 0, :
            ]

        support = jax.vmap(take)(sources, begins)
        selector = (basis_row[:, None] == jnp.arange(basis_count, dtype=jnp.int32)[None, :]).astype(
            jnp.float32
        ) * quad_row[:, None]
        aggregate = jnp.einsum(
            "kb,kcj->bcj", selector, support, precision=lax.Precision.HIGHEST
        ).astype(jnp.bfloat16)
        return lax.dot_general(
            disco_weight,
            aggregate,
            (((0, 1), (0, 1)), ((), ())),
            preferred_element_type=jnp.float32,
        )

    row_count = disco_dlat.shape[0]
    stacked = lax.map(
        one_row,
        (jnp.arange(row_count, dtype=jnp.int32), disco_dlat, disco_dlon, disco_basis, disco_quad),
    )
    return jnp.transpose(stacked, (1, 0, 2))


def per_device(
    grid_field,
    disco_dlat,
    disco_dlon,
    disco_basis,
    disco_quad,
    disco_weight,
    norm_gain,
    spectral_filter,
    mix_weight,
):
    lat_count = lax.axis_size("lat")
    lon_count = lax.axis_size("lon")
    channels, lat_local, lon_local = grid_field.shape
    lat_total = lat_local * lat_count
    lon_total = lon_local * lon_count
    mode_count = M_DEV * lat_count
    chan_local = channels // lon_count
    lat_index = lax.axis_index("lat")
    lon_index = lax.axis_index("lon")
    wrapped = padded_2(grid_field, (("lat", 1), ("lon", 2)), HALO)
    global_rows = lat_index * lat_local + jnp.arange(lat_local + 2 * HALO, dtype=jnp.int32) - HALO
    inside = (global_rows >= 0) & (global_rows < lat_total)
    padded = jnp.where(inside[None, :, None], wrapped, 0.0)
    after_conv = grid_field + disco_rows(
        padded, disco_dlat, disco_dlon, disco_basis, disco_quad, disco_weight, lon_local
    )
    mean_square = jnp.mean(after_conv * after_conv, axis=0, keepdims=True)
    normed = after_conv * lax.rsqrt(mean_square + 1e-06) * norm_gain[:, None, None]
    lon_pos = jnp.arange(lon_total, dtype=jnp.int32)
    mode_pos = jnp.arange(mode_count, dtype=jnp.int32)
    phase = (lon_pos[:, None] * mode_pos[None, :] % lon_total).astype(jnp.float32) * (
        2.0 * math.pi / lon_total
    )
    cos_part = jnp.cos(phase)
    sin_part = jnp.sin(phase)
    forward_table = jnp.concatenate([cos_part, -sin_part], axis=1) * (2.0 * math.pi / lon_total)
    mode_weight = jnp.where(mode_pos == 0, 1.0, 2.0).astype(jnp.float32)[None, :]
    inverse_table = jnp.transpose(
        jnp.concatenate([cos_part * mode_weight, -sin_part * mode_weight], axis=1)
    )
    portion = lax.all_to_all(normed, "lon", split_axis=0, concat_axis=2, tiled=True)
    result = jnp.einsum("crj,jq->qcr", portion, forward_table, precision=lax.Precision.HIGHEST)
    fourier = result.reshape(2, mode_count, portion.shape[0], portion.shape[1])
    table = legendre_table(lat_index * M_DEV, M_DEV, mode_count, mode_count, lat_total)
    lat_pos = jnp.arange(lat_total, dtype=jnp.float32)
    quad_weight = math.pi / lat_total * jnp.sin(math.pi * (lat_pos + 0.5) / lat_total)
    local_filter = lax.dynamic_slice_in_dim(spectral_filter, lon_index * chan_local, chan_local, 0)
    weighted = lax.all_to_all(fourier, "lat", split_axis=1, concat_axis=3, tiled=True) * quad_weight
    spectra = jnp.einsum("rmck,lmk->rmcl", weighted, table, precision=lax.Precision.HIGHEST)
    filtered = spectra * local_filter[None, None]
    synthesis = jnp.einsum("rmcl,lmk->rmck", filtered, table, precision=lax.Precision.HIGHEST)
    returned = lax.all_to_all(synthesis, "lat", split_axis=3, concat_axis=1, tiled=True)
    wave_field = jnp.einsum(
        "qcr,qj->crj",
        returned.reshape(2 * mode_count, chan_local, lat_local),
        inverse_table,
        precision=lax.Precision.HIGHEST,
    )
    activated_local = jax.nn.gelu(wave_field, approximate=True).astype(jnp.bfloat16)
    activated = lax.all_to_all(activated_local, "lon", split_axis=2, concat_axis=0, tiled=True)
    mixed = lax.dot_general(
        mix_weight, activated, (((0,), (0,)), ((), ())), preferred_element_type=jnp.float32
    )
    return after_conv + mixed


def solution(mesh):
    placed = (
        P(None, "lat", "lon"),
        P("lat", None),
        P("lat", None),
        P("lat", None),
        P("lat", None),
        P(),
        P(),
        P(),
        P(),
    )
    return jax.shard_map(
        per_device, mesh=mesh, in_specs=placed, out_specs=P(None, "lat", "lon"), check_vma=False
    )
```

profile of v0, /device:TPU:0, one launch (start us, length us, event | category | flops | bytes accessed | tf_op | source)
XLA Modules:
  0.0 368.7 jit_solution(16414946515964665758)
XLA Ops:
  9.4 14.1 %collective-permute-done = f32[384,2,128]{0,1,2:T(2,128)} collective-permute-done((f32[384,2,128]{0,1,2:T(2,128)}, f32[384,2,128]{0,1,2:T(2,128)}, u32[]{:S(2)}, u32[]{:S(2)}) %collective-permute-start) | collective-permute-done | bytes 393248 | tf_op jit(solution)/shard_map/ppermute | solution.py:19
  32.9 146.3 %while.33 = (s32[]{:T(128)}, f32[8,384,128]{1,2,0:T(8,128)}, s32[8,16]{1,0:T(8,128)}, f32[8,16]{1,0:T(8,128)}, s32[8]{0:T(128)S(1)}, /*index=5*/s32[8,16]{1,0:T(...) while((s32[]{:T(128)}, f32[8,384,128]{1,2,0:T(8,128)}, ...), condition=%wide.region_1.2_spmd, body=%wide.region_0.1_spmd.sunk | while | flops 188940624 | bytes 22611376 | solution.py:107
  35.0 6.6 %gather_fusion = f32[16,384,128]{1,0,2:T(8,128)} fusion(f32[384,12,132]{0,1,2:T(8,128)S(1)} %get-tuple-element.853, s32[16]{0:T(128)S(1)} %or_bitcast_fusion.2), kind=kCustom, calls=%fused_computation.clone.1 | custom fusion | bytes 6291648 | tf_op jit(solution)/shard_map/while/body/eval_jaxpr/vmap()/gather | solution.py:88
  41.5 3.6 copy.119
  46.5 3.6 convolution_convert_fusion.2
  53.3 6.6 %gather_fusion = f32[16,384,128]{1,0,2:T(8,128)} fusion(f32[384,12,132]{0,1,2:T(8,128)S(1)} %get-tuple-element.853, s32[16]{0:T(128)S(1)} %or_bitcast_fusion.2), kind=kCustom, calls=%fused_computation.clone.1 | custom fusion | bytes 6291648 | tf_op jit(solution)/shard_map/while/body/eval_jaxpr/vmap()/gather | solution.py:88
  59.8 3.6 copy.119
  64.8 3.6 convolution_convert_fusion.2
  71.6 6.6 %gather_fusion = f32[16,384,128]{1,0,2:T(8,128)} fusion(f32[384,12,132]{0,1,2:T(8,128)S(1)} %get-tuple-element.853, s32[16]{0:T(128)S(1)} %or_bitcast_fusion.2), kind=kCustom, calls=%fused_computation.clone.1 | custom fusion | bytes 6291648 | tf_op jit(solution)/shard_map/while/body/eval_jaxpr/vmap()/gather | solution.py:88
  78.1 3.6 copy.119
  83.1 3.6 convolution_convert_fusion.2
  89.8 6.6 %gather_fusion = f32[16,384,128]{1,0,2:T(8,128)} fusion(f32[384,12,132]{0,1,2:T(8,128)S(1)} %get-tuple-element.853, s32[16]{0:T(128)S(1)} %or_bitcast_fusion.2), kind=kCustom, calls=%fused_computation.clone.1 | custom fusion | bytes 6291648 | tf_op jit(solution)/shard_map/while/body/eval_jaxpr/vmap()/gather | solution.py:88
  96.4 3.6 copy.119
  101.4 3.6 convolution_convert_fusion.2
  108.1 6.6 %gather_fusion = f32[16,384,128]{1,0,2:T(8,128)} fusion(f32[384,12,132]{0,1,2:T(8,128)S(1)} %get-tuple-element.853, s32[16]{0:T(128)S(1)} %or_bitcast_fusion.2), kind=kCustom, calls=%fused_computation.clone.1 | custom fusion | bytes 6291648 | tf_op jit(solution)/shard_map/while/body/eval_jaxpr/vmap()/gather | solution.py:88
  114.7 3.6 copy.119
  119.7 3.6 convolution_convert_fusion.2
  126.4 6.6 %gather_fusion = f32[16,384,128]{1,0,2:T(8,128)} fusion(f32[384,12,132]{0,1,2:T(8,128)S(1)} %get-tuple-element.853, s32[16]{0:T(128)S(1)} %or_bitcast_fusion.2), kind=kCustom, calls=%fused_computation.clone.1 | custom fusion | bytes 6291648 | tf_op jit(solution)/shard_map/while/body/eval_jaxpr/vmap()/gather | solution.py:88
  132.9 3.6 copy.119
  144.7 6.6 %gather_fusion = f32[16,384,128]{1,0,2:T(8,128)} fusion(f32[384,12,132]{0,1,2:T(8,128)S(1)} %get-tuple-element.853, s32[16]{0:T(128)S(1)} %or_bitcast_fusion.2), kind=kCustom, calls=%fused_computation.clone.1 | custom fusion | bytes 6291648 | tf_op jit(solution)/shard_map/while/body/eval_jaxpr/vmap()/gather | solution.py:88
  151.2 3.6 copy.119
  156.2 3.6 convolution_convert_fusion.2
  162.9 6.6 %gather_fusion = f32[16,384,128]{1,0,2:T(8,128)} fusion(f32[384,12,132]{0,1,2:T(8,128)S(1)} %get-tuple-element.853, s32[16]{0:T(128)S(1)} %or_bitcast_fusion.2), kind=kCustom, calls=%fused_computation.clone.1 | custom fusion | bytes 6291648 | tf_op jit(solution)/shard_map/while/body/eval_jaxpr/vmap()/gather | solution.py:88
  169.5 3.6 copy.119
  174.5 3.6 convolution_convert_fusion.2
  184.9 3.7 %all-to-all-start = ((f32[384,8,128]{2,1,0:T(8,128)}), f32[384,8,128]{2,1,0:T(8,128)S(1)}, u32[]{:S(2)}, u32[]{:S(2)}) async-start(f32[384,8,128]{2,1,0:T(8,128)} %copy.83), calls=%async_computation | async-start | bytes 3145728 | tf_op jit(solution)/shard_map/all_to_all | solution.py:155
  192.8 15.7 %all-to-all-done = f32[384,8,128]{2,1,0:T(8,128)S(1)} async-done(((f32[384,8,128]{2,1,0:T(8,128)}), f32[384,8,128]{2,1,0:T(8,128)S(1)}, u32[]{:S(2)}, u32[]{:S(2)}) %all-to-all-start) | async-done | bytes 1572896 | tf_op jit(solution)/shard_map/all_to_all | solution.py:155
  216.6 4.6 %all-to-all-start.1 = ((f32[2,64,96,8]{2,3,0,1:T(8,128)}), f32[2,64,96,8]{2,3,0,1:T(8,128)S(1)}, u32[]{:S(2)}, u32[]{:S(2)}) async-start(f32[2,64,96,8]{2,3,0,1:T(8,128)} %copy.85), calls=%async_computation.1 | async-start | bytes 1048576 | tf_op jit(solution)/shard_map/all_to_all | solution.py:162
  221.3 95.3 %while.34 = (s32[]{:T(128)}, f32[8,64]{1,0:T(8,128)S(1)}, f32[8,64]{1,0:T(8,128)S(1)}, f32[8,8,8,64]{3,2,1,0:T(8,128)S(1)}, s32[8,8]{1,0:T(8,128)S(1)}, /*index=...) while((s32[]{:T(128)}, f32[8,64]{1,0:T(8,128)S(1)}, ...), condition=%wide.region_4.5_spmd.clone.clone.clone.clone, body=%wide.region_3.4_spmd.clone.clone.clone.clone.sunk | while | flops 93138 | bytes 238507 | solution.py:71
  320.2 6.0 %all-to-all-start.2 = ((f32[2,8,96,64]{2,0,1,3:T(2,128)}), f32[2,8,96,64]{2,0,1,3:T(2,128)S(1)}, u32[]{:S(2)}, u32[]{:S(2)}) async-start(f32[2,8,96,64]{2,0,1,3:T(2,128)} %copy.91), calls=%async_computation.2 | async-start | bytes 1048576 | tf_op jit(solution)/shard_map/all_to_all | solution.py:166
  327.3 12.6 %all-to-all-done.2 = f32[2,8,96,64]{2,0,1,3:T(2,128)S(1)} async-done(((f32[2,8,96,64]{2,0,1,3:T(2,128)}), f32[2,8,96,64]{2,0,1,3:T(2,128)S(1)}, u32[]{:S(2)}, u32[]{:S(2)}) %all-to-all-start.2) | async-done | bytes 393248 | tf_op jit(solution)/shard_map/all_to_all | solution.py:166
  345.2 17.6 %all_to_all.69 = bf16[96,8,512]{0,1,2:T(8,128)(2,1)} all-to-all(bf16[96,8,512]{0,1,2:T(8,128)(2,1)S(1)} %copy.94), channel_id=1, replica_groups=mesh['lat'=8,'lon'=4] {'lon'}, dimensions={2} | all-to-all | bytes 1572864 | tf_op jit(solution)/shard_map/all_to_all | solution.py:174
  (349 shorter events, 140.2 us)
Async XLA Ops:
  0.0 365.0 %copy-start = (bf16[384,384]{1,0:T(8,128)(2,1)S(1)}, bf16[384,384]{1,0:T(8,128)(2,1)}, u32[]{:S(2)}) copy-start(bf16[384,384]{1,0:T(8,128)(2,1)} %param.21) | copy-start | bytes 884740
  2.0 24.4 %copy-start.3 = (f32[384,8,128]{0,1,2:T(8,128)}, f32[384,8,128]{0,1,2:T(8,128)S(1)}, u32[]{:S(2)}) copy-start(f32[384,8,128]{0,1,2:T(8,128)S(1)} %copy.78) | copy-start | bytes 4718596
  3.3 24.9 %copy-start.4 = (f32[384,8,128]{2,1,0:T(8,128)S(1)}, f32[384,8,128]{2,1,0:T(8,128)}, u32[]{:S(2)}) copy-start(f32[384,8,128]{2,1,0:T(8,128)} %param.13) | copy-start | bytes 4718596
  3.3 20.1 %collective-permute-start = (f32[384,2,128]{0,1,2:T(2,128)}, f32[384,2,128]{0,1,2:T(2,128)}, u32[]{:S(2)}, u32[]{:S(2)}) collective-permute-start(f32[384,2,128]{0,1,2:T(2,128)} %get-tuple-element.570), channel_id=1, source_target_pairs={{0,4},{4,8},{8,12},{12,16},{16,20},{20,24},{24,28},{28,0},{1,5},{5... | collective-permute-start | bytes 1179656 | tf_op jit(solution)/shard_map/ppermute | solution.py:19
  6.3 19.3 %collective-permute-start.1 = (f32[384,2,128]{0,1,2:T(2,128)}, f32[384,2,128]{0,1,2:T(2,128)}, u32[]{:S(2)}, u32[]{:S(2)}) collective-permute-start(f32[384,2,128]{0,1,2:T(2,128)} %get-tuple-element.571), channel_id=1, source_target_pairs={{4,0},{8,4},{12,8},{16,12},{20,16},{24,20},{28,24},{0,28},{5,1},{9... | collective-permute-start | bytes 1179656 | tf_op jit(solution)/shard_map/ppermute | solution.py:21
  26.4 3.6 collective-permute-start.2
  26.5 4.1 %collective-permute-start.3 = (f32[384,12,2]{0,1,2:T(8,128)S(1)}, f32[384,12,2]{0,1,2:T(8,128)}, u32[]{:S(2)}, u32[]{:S(2)}) collective-permute-start(f32[384,12,2]{0,1,2:T(8,128)S(1)} %get-tuple-element.569), channel_id=1, source_target_pairs={{1,0},{2,1},{3,2},{0,3},{5,4},{6,5},{7,6},{4,7},{9,8},{10,9},{11,1... | collective-permute-start | bytes 110600 | tf_op jit(solution)/shard_map/ppermute | solution.py:21
  30.0 0.6 copy-start.6
  46.5 3.6 copy-start.1
  64.8 3.6 copy-start.1
  83.1 3.6 copy-start.1
  101.4 3.6 copy-start.1
  119.7 3.6 copy-start.1
  137.9 3.6 copy-start.1
  156.2 3.6 copy-start.1
  174.5 3.6 copy-start.1
  179.2 2.4 copy-start.2
  179.2 2.4 copy-start.7
  184.9 23.6 %all-to-all-start = ((f32[384,8,128]{2,1,0:T(8,128)}), f32[384,8,128]{2,1,0:T(8,128)S(1)}, u32[]{:S(2)}, u32[]{:S(2)}) async-start(f32[384,8,128]{2,1,0:T(8,128)} %copy.83), calls=%async_computation | async-start | bytes 3145728 | tf_op jit(solution)/shard_map/all_to_all | solution.py:155
  215.5 5.7 %copy-start.5 = (f32[8,8,8,64]{3,2,1,0:T(8,128)S(1)}, f32[8,8,8,64]{3,2,1,0:T(8,128)}, u32[]{:S(2)}) copy-start(f32[8,8,8,64]{3,2,1,0:T(8,128)} %custom-call.6) | copy-start | bytes 393220
  216.6 101.1 %all-to-all-start.1 = ((f32[2,64,96,8]{2,3,0,1:T(8,128)}), f32[2,64,96,8]{2,3,0,1:T(8,128)S(1)}, u32[]{:S(2)}, u32[]{:S(2)}) async-start(f32[2,64,96,8]{2,3,0,1:T(8,128)} %copy.85), calls=%async_computation.1 | async-start | bytes 1048576 | tf_op jit(solution)/shard_map/all_to_all | solution.py:162
  320.2 19.7 %all-to-all-start.2 = ((f32[2,8,96,64]{2,0,1,3:T(2,128)}), f32[2,8,96,64]{2,0,1,3:T(2,128)S(1)}, u32[]{:S(2)}, u32[]{:S(2)}) async-start(f32[2,8,96,64]{2,0,1,3:T(2,128)} %copy.91), calls=%async_computation.2 | async-start | bytes 1048576 | tf_op jit(solution)/shard_map/all_to_all | solution.py:166
where the time goes:
time: 371 us; the launch traced here: 369 us
  local copies, waits for them, and re-layouts  126 us (34%)
  other arithmetic  63.9 us (17%)
  loops' own time  47.8 us (13%)
  matrix products  46.6 us (13%)
  waiting for transfers between devices  44.6 us (12%)
  starting transfers between devices  22.2 us (6%)
  blocking collectives  17.6 us (5%)
    gather x16, local copies, waits for them, and re-layouts, take(): lax.dynamic_slice(padded, (zero_index, source, begin), (channels, 1, width))  81.2 us
    another operation x1, loops' own time, legendre_table(): lax.scan(advance, (empty, empty), jnp.arange(degrees, dtype=jnp.int32), u...  42.2 us
    gt x64, other arithmetic, advance(): degree > orders[:, None]  40.5 us
    dot_general x8, matrix products, one_row(): jnp.einsum('kb,kcj->bcj', selector, support, precision=lax.Precision.HIGH...  28.7 us
    all_to_all x1, blocking collectives, per_device(): lax.all_to_all(activated_local, 'lon', split_axis=2, concat_axis=0, tiled...  17.6 us
    all_to_all x1, waiting for transfers between devices, per_device(): lax.all_to_all(normed, 'lon', split_axis=0, concat_axis=2, tiled=True)  15.7 us
    ppermute x2, waiting for transfers between devices, padded_2(): lax.ppermute(tail, axis, [(i, (i + 1) % count) for i in range(count)])  14.1 us
    all_to_all x1, waiting for transfers between devices, per_device(): lax.all_to_all(synthesis, 'lat', split_axis=3, concat_axis=1, tiled=True)  12.6 us
  transfers between devices with their start and end apart: 7, of which 5 were waited for; matrix products, arithmetic and copies ran while one was open for 17% of the time, Pallas kernels for 0%

commit v1 on v0

v1 whole, which is shorter than its diff:
```python
import functools
import math

import jax
import jax.numpy as jnp
import numpy as np
from jax import lax
from jax.experimental import pallas as pl
from jax.experimental.pallas import tpu as pltpu
from jax.sharding import PartitionSpec as P

M_DEV = 8
HALO = 2
PAD = 16
LANES = 128
MESH = pl.DeviceIdType.MESH
VM = pl.BlockSpec(memory_space=pltpu.VMEM)
SM = pl.BlockSpec(memory_space=pltpu.SMEM)


def halo_kernel(lat_n, lon_n, x_ref, xp_ref, xt_ref, send_sem, recv_sem):
    rows, width, chans = xt_ref.shape
    lat, lon = lax.axis_index("lat"), lax.axis_index("lon")
    up, down = lax.rem(lat + lat_n - 1, lat_n), lax.rem(lat + 1, lat_n)
    left, right = lax.rem(lon + lon_n - 1, lon_n), lax.rem(lon + 1, lon_n)
    barrier = pltpu.get_barrier_semaphore()
    peers = [(a, b) for a in (up, lat, down) for b in (left, lon, right)]
    peers.pop(4)
    for peer in peers:
        pl.semaphore_signal(barrier, inc=1, device_id=peer, device_id_type=MESH)

    def turn(row):
        cells = x_ref[:, row, :].T
        xt_ref[row] = cells
        xp_ref[row + HALO, PAD : PAD + width, :] = cells.astype(jnp.bfloat16)

    edge = list(range(HALO)) + list(range(rows - HALO, rows))
    for row in edge:
        turn(row)
    pl.semaphore_wait(barrier, len(peers))
    row_spans = {
        -1: (HALO, rows + HALO, HALO),
        0: (HALO, HALO, rows),
        1: (rows, 0, HALO),
    }
    col_spans = {
        -1: (PAD, PAD + width, PAD),
        0: (PAD, PAD, width),
        1: (width, 0, PAD),
    }
    copies = []

    def send(dv, dh):
        peer = ({-1: up, 0: lat, 1: down}[dv], {-1: left, 0: lon, 1: right}[dh])
        rs, rd, rn = row_spans[dv]
        cs, cd, cn = col_spans[dh]
        index = (dv + 1) * 3 + dh + 1
        copy = pltpu.make_async_remote_copy(
            src_ref=xp_ref.at[rs : rs + rn, cs : cs + cn, :],
            dst_ref=xp_ref.at[rd : rd + rn, cd : cd + cn, :],
            send_sem=send_sem.at[index],
            recv_sem=recv_sem.at[index],
            device_id=peer,
            device_id_type=MESH,
        )
        copy.start()
        copies.append(copy)

    for dv in (-1, 1):
        for dh in (0, -1, 1):
            send(dv, dh)
    for row in range(HALO, rows - HALO):
        turn(row)
    for dh in (-1, 1):
        send(0, dh)
    for copy in copies:
        copy.wait()


def conv_kernel(
    src_ref, begin_ref, basis_ref, quad_ref, xp_ref, xt_ref, w_ref, gain_ref, table_ref,
    ac_ref, fp_ref, y_ref,
):
    rows, width, chans = xt_ref.shape
    basis_count = w_ref.shape[0]
    taps = src_ref.shape[1]
    slabs = chans // LANES
    tall = xp_ref.shape[1]

    @pl.loop(0, rows + 2 * HALO)
    def _(row):
        cells = xp_ref[row]
        for b in range(basis_count):
            mixed = jnp.dot(cells, w_ref[b], preferred_element_type=jnp.float32)
            for c in range(slabs):
                y_ref[b // 2, row, c, pl.ds(b % 2, tall, stride=2), :] = mixed[
                    :, c * LANES : (c + 1) * LANES
                ]

    step = 32

    @pl.loop(0, rows)
    def _(row):
        @pl.loop(0, width // step)
        def _(part):
            base = pl.multiple_of(part * step, step)
            totals = [
                xt_ref[row, pl.ds(base, step), c * LANES : (c + 1) * LANES] for c in range(slabs)
            ]
            for k in range(taps):
                basis, source, scale = basis_ref[row, k], src_ref[row, k], quad_ref[row, k]
                begin = 2 * (base + begin_ref[row, k]) + (basis & 1)
                for c in range(slabs):
                    totals[c] = totals[c] + scale * y_ref[
                        basis >> 1, source, c, pl.ds(begin, step, stride=2), :
                    ]
            for c in range(slabs):
                ac_ref[row, pl.ds(base, step), c * LANES : (c + 1) * LANES] = totals[c]

        cells = ac_ref[row]
        mean = jnp.mean(cells * cells, axis=1, keepdims=True)
        normed = cells * lax.rsqrt(mean + 1e-06) * gain_ref[...]
        fp_ref[row] = jnp.dot(
            table_ref[...], normed.astype(jnp.bfloat16), preferred_element_type=jnp.float32
        ).astype(jnp.bfloat16)


def spectral_kernel(
    lat_n, lon_n, fp_ref, ac_ref, ab_ref, seed_ref, undo_ref, quadw_ref, filt_ref,
    out_ref,
    recv1, red, snd2, recv2, legendre, back, snd3,
    s1, r1, s2, r2, s3, r3, s4, r4,
):
    rows, all_q, chans = fp_ref.shape
    group = all_q // lon_n
    count = group // lat_n
    degrees, _, nlat = ac_ref.shape
    wire = snd2.dtype
    lat, lon = lax.axis_index("lat"), lax.axis_index("lon")

    barrier = pltpu.get_barrier_semaphore()
    for off in range(1, lon_n):
        pl.semaphore_signal(
            barrier, inc=1, device_id=(lat, lax.rem(lon + off, lon_n)), device_id_type=MESH
        )
    for off in range(1, lat_n):
        pl.semaphore_signal(
            barrier, inc=1, device_id=(lax.rem(lat + off, lat_n), lon), device_id_type=MESH
        )
    pl.semaphore_wait(barrier, lon_n + lat_n - 2)

    first = []
    for off in range(1, lon_n):
        peer = lax.rem(lon + off, lon_n)
        copy = pltpu.make_async_remote_copy(
            src_ref=fp_ref.at[:, pl.ds(pl.multiple_of(peer * group, group), group), :],
            dst_ref=recv1.at[off - 1],
            send_sem=s1.at[off - 1],
            recv_sem=r1.at[off - 1],
            device_id=(lat, peer),
            device_id_type=MESH,
        )
        copy.start()
        first.append(copy)

    zero = undo_ref[...] * 0.0

    def advance(degree, pair):
        previous, older = pair
        current = ac_ref[degree] * previous - ab_ref[degree] * older + seed_ref[degree]
        legendre[degree] = current * undo_ref[...]
        return (current, previous)

    lax.fori_loop(0, degrees, advance, (zero, zero), unroll=4)

    for copy in first:
        copy.wait()
    mine = pl.ds(pl.multiple_of(lon * group, group), group)
    for row in range(rows):
        total = fp_ref[row, mine, :].astype(jnp.float32)
        for off in range(1, lon_n):
            total = total + recv1[off - 1, row].astype(jnp.float32)
        red[:, row, :] = total
    for d in range(lat_n):
        snd2[d] = red[d * count : (d + 1) * count].reshape(count * rows, chans).astype(wire)

    second = []
    for off in range(1, lat_n):
        peer = lax.rem(lat + off, lat_n)
        copy = pltpu.make_async_remote_copy(
            src_ref=snd2.at[peer],
            dst_ref=recv2.at[lat],
            send_sem=s2.at[off - 1],
            recv_sem=r2.at[off - 1],
            device_id=(peer, lon),
            device_id_type=MESH,
        )
        copy.start()
        second.append(copy)
    recv2[lat] = snd2[lat]
    tables = [legendre[:, t, :] for t in range(count)]
    for copy in second:
        copy.wait()

    for t in range(count):
        cells = recv2[:, t * rows : (t + 1) * rows, :].astype(jnp.float32)
        cells = cells.reshape(lat_n * rows, chans).astype(jnp.bfloat16)
        analysis = (tables[t] * quadw_ref[...]).astype(jnp.bfloat16)
        spectra = jnp.dot(analysis, cells, preferred_element_type=jnp.float32)
        filtered = (spectra * filt_ref[...]).astype(jnp.bfloat16)
        result = jnp.dot(
            tables[t].T.astype(jnp.bfloat16), filtered, preferred_element_type=jnp.float32
        )
        back[:, t * rows : (t + 1) * rows, :] = result.reshape(lat_n, rows, chans)
    for d in range(lat_n):
        snd3[d] = back[d].astype(wire)

    third = []
    for off in range(1, lat_n):
        peer = lax.rem(lat + off, lat_n)
        copy = pltpu.make_async_remote_copy(
            src_ref=snd3.at[peer],
            dst_ref=out_ref.at[lon, lat],
            send_sem=s3.at[off - 1],
            recv_sem=r3.at[off - 1],
            device_id=(peer, lon),
            device_id_type=MESH,
        )
        copy.start()
        third.append(copy)
    out_ref[lon, lat] = snd3[lat]

    fourth = []

    def spread(source, slot):
        for off in range(1, lon_n):
            peer = lax.rem(lon + off, lon_n)
            copy = pltpu.make_async_remote_copy(
                src_ref=out_ref.at[lon, source],
                dst_ref=out_ref.at[lon, source],
                send_sem=s4.at[slot, off - 1],
                recv_sem=r4.at[slot, off - 1],
                device_id=(lat, peer),
                device_id_type=MESH,
            )
            copy.start()
            fourth.append(copy)

    spread(lat, 0)
    for off in range(1, lat_n):
        third[off - 1].wait()
        spread(lax.rem(lat + lat_n - off, lat_n), off)
    for copy in fourth:
        copy.wait()


def output_kernel(syn_ref, ac_ref, table_ref, mix_ref, o_ref, wide):
    rows, width, chans = ac_ref.shape
    all_q = table_ref.shape[1]
    wide[...] = syn_ref[...].astype(jnp.float32).reshape(all_q, rows, chans)
    for row in range(rows):
        waves = wide[:, row, :].astype(jnp.bfloat16)
        field = jnp.dot(table_ref[...], waves, preferred_element_type=jnp.float32)
        active = jax.nn.gelu(field, approximate=True).astype(jnp.bfloat16)
        total = ac_ref[row] + jnp.dot(active, mix_ref[...], preferred_element_type=jnp.float32)
        o_ref[:, row, :] = total.T


def per_device(
    grid_field,
    disco_dlat,
    disco_dlon,
    disco_basis,
    disco_quad,
    disco_weight,
    norm_gain,
    spectral_filter,
    mix_weight,
):
    lat_n = lax.axis_size("lat")
    lon_n = lax.axis_size("lon")
    chans, rows, width = grid_field.shape
    nlat, nlon = rows * lat_n, width * lon_n
    modes = M_DEV * lat_n
    all_q = 2 * modes
    degrees = spectral_filter.shape[1]
    group = all_q // lon_n
    count = group // lat_n
    basis_count = disco_weight.shape[0]
    lat, lon = lax.axis_index("lat"), lax.axis_index("lon")
    f32, bf16 = jnp.float32, jnp.bfloat16

    xp, xt = pl.pallas_call(
        functools.partial(halo_kernel, lat_n, lon_n),
        out_shape=(
            jax.ShapeDtypeStruct((rows + 2 * HALO, width + 2 * PAD, chans), bf16),
            jax.ShapeDtypeStruct((rows, width, chans), f32),
        ),
        in_specs=[VM],
        out_specs=(VM, VM),
        scratch_shapes=[pltpu.SemaphoreType.DMA((9,)), pltpu.SemaphoreType.DMA((9,))],
        compiler_params=pltpu.CompilerParams(collective_id=0, has_side_effects=True),
    )(grid_field)

    q_pos = jnp.arange(all_q, dtype=jnp.int32)
    j_pos = lon * width + jnp.arange(width, dtype=jnp.int32)
    turns = (j_pos[:, None] * (q_pos // 2)[None, :] + (q_pos % 2)[None, :] * (nlon // 4)) % nlon
    wave = jnp.cos(turns.astype(f32) * (2.0 * math.pi / nlon))
    forward = (wave.T * (2.0 * math.pi / nlon)).astype(bf16)
    inverse = (wave * jnp.where(q_pos < 2, 1.0, 2.0)[None, :]).astype(bf16)

    row_pos = jnp.arange(rows, dtype=jnp.int32)[:, None]
    source = row_pos + disco_dlat
    globally = lat * rows + source
    quad = jnp.where((globally >= 0) & (globally < nlat), disco_quad, 0.0)

    after_conv, partial = pl.pallas_call(
        conv_kernel,
        out_shape=(
            jax.ShapeDtypeStruct((rows, width, chans), f32),
            jax.ShapeDtypeStruct((rows, all_q, chans), bf16),
        ),
        in_specs=[SM] * 4 + [VM] * 5,
        out_specs=(VM, VM),
        scratch_shapes=[
            pltpu.VMEM(
                (
                    (basis_count + 1) // 2,
                    rows + 2 * HALO,
                    chans // LANES,
                    2 * (width + 2 * PAD),
                    LANES,
                ),
                f32,
            )
        ],
    )(
        source + HALO, disco_dlon + PAD, disco_basis, quad,
        xp, xt, disco_weight, norm_gain[None, :], forward,
    )

    lat_pos = jnp.arange(nlat, dtype=f32)
    colatitude = math.pi * (lat_pos + 0.5) / nlat
    cosine, sine = jnp.cos(colatitude), jnp.sin(colatitude)
    order = ((lon * group + lat * count + jnp.arange(count, dtype=jnp.int32)) // 2).astype(f32)
    counters = jnp.arange(1, modes, dtype=f32)
    logs = jnp.log((2.0 * counters - 1.0) / (2.0 * counters))
    log_product = jnp.sum(jnp.where(counters[None, :] <= order[:, None], logs[None, :], 0.0), 1)
    om = order[:, None]
    log_seed = (
        0.5 * (jnp.log((2.0 * om + 1.0) / (4.0 * math.pi)) + log_product[:, None])
        + om * jnp.log(sine)[None, :]
    )
    rescale = jnp.clip(-log_seed, 0.0, 80.0)
    seed_value = jnp.exp(log_seed + rescale)
    undo = jnp.exp(-rescale)
    ell = jnp.arange(degrees, dtype=f32)[:, None, None]
    om3 = order[None, :, None]
    a = jnp.sqrt(jnp.maximum(4.0 * ell**2 - 1.0, 1.0) / jnp.maximum(ell**2 - om3**2, 1.0))
    b = jnp.sqrt(
        jnp.maximum((ell - 1.0) ** 2 - om3**2, 0.0)
        / jnp.maximum(4.0 * (ell - 1.0) ** 2 - 1.0, 1.0)
    )
    a = jnp.where(ell > om3, a, 0.0)
    a_cos = a * cosine[None, None, :]
    a_b = jnp.broadcast_to(a * b, a_cos.shape)
    seeds = jnp.where(ell == om3, seed_value[None], 0.0)
    quad_weight = (math.pi / nlat * sine)[None, :]

    wire = bf16 if (count * rows) % 16 == 0 else f32
    block = (lat_n, count * rows, chans)
    dma = pltpu.SemaphoreType.DMA
    synthesis = pl.pallas_call(
        functools.partial(spectral_kernel, lat_n, lon_n),
        out_shape=jax.ShapeDtypeStruct((lon_n,) + block, wire),
        in_specs=[VM] * 7,
        out_specs=VM,
        scratch_shapes=[
            pltpu.VMEM((lon_n - 1, rows, group, chans), bf16),
            pltpu.VMEM((group, rows, chans), f32),
            pltpu.VMEM(block, wire),
            pltpu.VMEM(block, wire),
            pltpu.VMEM((degrees, count, nlat), f32),
            pltpu.VMEM(block, f32),
            pltpu.VMEM(block, wire),
            dma((lon_n - 1,)), dma((lon_n - 1,)),
            dma((lat_n - 1,)), dma((lat_n - 1,)),
            dma((lat_n - 1,)), dma((lat_n - 1,)),
            dma((lat_n, lon_n - 1)), dma((lat_n, lon_n - 1)),
        ],
        compiler_params=pltpu.CompilerParams(collective_id=1, has_side_effects=True),
    )(partial, a_cos, a_b, seeds, undo, quad_weight, spectral_filter.T)

    return pl.pallas_call(
        output_kernel,
        out_shape=jax.ShapeDtypeStruct((chans, rows, width), f32),
        in_specs=[VM] * 4,
        out_specs=VM,
        scratch_shapes=[pltpu.VMEM((all_q, rows, chans), f32)],
    )(synthesis, after_conv, inverse, mix_weight)


def solution(mesh):
    placed = (
        P(None, "lat", "lon"),
        P("lat", None),
        P("lat", None),
        P("lat", None),
        P("lat", None),
        P(),
        P(),
        P(),
        P(),
    )
    return jax.shard_map(
        per_device, mesh=mesh, in_specs=placed, out_specs=P(None, "lat", "lon"), check_vma=False
    )
```

time: 371 us -> 83.8 us (0.23)
  local copies, waits for them, and re-layouts: 126 us -> 1.37 us
  Pallas kernels: 0 us -> 74.9 us
  other arithmetic: 63.9 us -> 7.2 us
  loops' own time: 47.8 us -> 0 us
  matrix products: 46.6 us -> 0 us
  waiting for transfers between devices: 44.6 us -> 0 us
  starting transfers between devices: 22.2 us -> 0 us
  blocking collectives: 17.6 us -> 0 us
    gather x16 -> x0, local copies, waits for them, and re-layouts: 81.2 us -> none  [take(): lax.dynamic_slice(padded, (zero_index, source, begin), (channels, 1, width))]
    pallas_call x0 -> x4, Pallas kernels: none -> 74.9 us  [the longest x1 34.9 us: per_device(): pl.pallas_call(functools.partial(spectral_kernel, lat_n, lon_n), out_shap...]
    another operation x2 -> x0, loops' own time: 47.8 us -> none  [the longest x1 42.2 us: legendre_table(): lax.scan(advance, (empty, empty), jnp.arange(degrees, dtype=jnp.int32), u...]
    dot_general x21 -> x0, matrix products: 46.6 us -> none  [the longest x8 28.7 us: one_row(): jnp.einsum('kb,kcj->bcj', selector, support, precision=lax.Precision.HIGH...]
    gt x64 -> x0, other arithmetic: 40.5 us -> none  [advance(): degree > orders[:, None]]
    all_to_all x3 -> x0, waiting for transfers between devices: 28.3 us -> none  [the longest x1 15.7 us: per_device(): lax.all_to_all(normed, 'lon', split_axis=0, concat_axis=2, tiled=True)]
    all_to_all x1 -> x0, blocking collectives: 17.6 us -> none  [per_device(): lax.all_to_all(activated_local, 'lon', split_axis=2, concat_axis=0, tiled...]
    ppermute x4 -> x0, waiting for transfers between devices: 16.3 us -> none  [the longest x2 14.1 us: padded_2(): lax.ppermute(tail, axis, [(i, (i + 1) % count) for i in range(count)])]
  transfers between devices with their start and end apart: 7 -> 0, of which waited for: 5 -> 0; matrix products, arithmetic and copies ran while one was open for 17% -> 0% of each run, Pallas kernels for 0% -> 0%
where the time goes in v1:
time: 83.8 us; the launch traced here: 83.6 us
  Pallas kernels  74.9 us (89%)
  other arithmetic  7.2 us (9%)
  local copies, waits for them, and re-layouts  1.37 us (2%)
    pallas_call x1, Pallas kernels, per_device(): pl.pallas_call(functools.partial(spectral_kernel, lat_n, lon_n), out_shap...  34.9 us
    pallas_call x1, Pallas kernels, per_device(): pl.pallas_call(functools.partial(halo_kernel, lat_n, lon_n), out_shape=(j...  20.1 us
    pallas_call x1, Pallas kernels, per_device(): pl.pallas_call(conv_kernel, out_shape=(jax.ShapeDtypeStruct((rows, width,...  13.6 us
    pallas_call x1, Pallas kernels, per_device(): pl.pallas_call(output_kernel, out_shape=jax.ShapeDtypeStruct((chans, rows...  6.28 us

profile of v1, /device:TPU:0, one launch (start us, length us, event | category | flops | bytes accessed | tf_op | source)
XLA Modules:
  0.0 83.6 jit_solution(7185530243751601913)
XLA Ops:
  0.0 0.0 copy-start
  0.0 1.3 %fusion.12 = (s32[8,16]{1,0:T(8,128)}, s32[8,16]{1,0:T(8,128)}) fusion(s32[8,16]{1,0:T(8,128)} %param.10, s32[8,16]{1,0:T(8,128)} %param.11), kind=kLoop, calls=%fused_computation.26 | loop fusion | flops 384 | bytes 2048 | tf_op jit(solution)/shard_map/add | solution.py:338
  1.3 1.3 %and_select_fusion.quad_ref = f32[8,16]{1,0:T(8,128)} fusion(f32[8,16]{1,0:T(8,128)} %param.13, s32[8,16]{1,0:T(8,128)} %param.10, s32[]{:T(128)S(6)} %mul.153), kind=kLoop, calls=%fused_computation.25 | loop fusion | flops 768 | bytes 1540 | tf_op jit(solution)/shard_map/jit(_where)/select_n | solution.py:315
  2.6 20.1 %shard_map.91 = (bf16[12,160,384]{2,1,0:T(8,128)(2,1)}, f32[8,128,384]{2,1,0:T(8,128)}) custom-call(f32[384,8,128]{2,1,0:T(8,128)} %x_ref.1), custom_call_target="tpu_custom_call" | custom-call | tf_op jit(solution)/shard_map/pallas_call | solution.py:293
  22.8 0.0 copy-done
  22.8 0.6 broadcast_in_dim.73.gain_ref
  23.4 1.2 %fusion.11 = (bf16[128,128]{1,0:T(8,128)(2,1)}, bf16[128,128]{1,0:T(8,128)(2,1)}) fusion(f32[128]{0:T(128)S(1)} %compare_select_fusion, s32[128]{0:T(128)S(1)} %get-tuple-element.20, s32[128]{0:T(128)S(1)} %get-tuple-element.19, s32[128]{0:T(128)S(1)} %iota_add_fusion.2), kind=kLoop, calls=%fused_computation.17 | loop fusion | flops 557056 | bytes 67584 | tf_op jit(solution)/shard_map/convert_element_type | solution.py:310
  24.6 13.6 %shard_map.92 = (f32[8,128,384]{2,1,0:T(8,128)}, bf16[8,128,384]{2,1,0:T(8,128)(2,1)}) custom-call(s32[8,16]{1,0:T(8,128)} %get-tuple-element.21.src_ref, s32[8,16]{1,0:T(8,128)} %get-tuple-element.22.begin_ref, s32[8,16]{1,0:T(8,128)} %basis_ref.1, f32[8,16]{1,0:T(8,128)} %and_select_fusion.quad_ref, bf16[12,160,384]{2,1,0:T(8,128)(2,1)} %get-tuple-element.9.xp_ref, ...), custom_call_target="tpu_custom_call" | custom-call | tf_op jit(solution)/shard_map/pallas_call | solution.py:317
  38.3 0.2 select_reduce_fusion
  38.5 0.1 sqrt_multiply_fusion
  38.6 0.8 broadcast_multiply_fusion.ac_ref
  39.4 0.8 broadcast_in_dim.75.ab_ref
  40.2 0.7 negate_exponential_fusion
  40.9 0.8 broadcast_select_fusion.seed_ref
  41.7 0.6 sine_multiply_fusion.quadw_ref
  42.3 34.9 %shard_map.93.syn_ref = bf16[4,8,32,384]{3,2,1,0:T(8,128)(2,1)} custom-call(bf16[8,128,384]{2,1,0:T(8,128)(2,1)} %get-tuple-element.11.fp_ref, f32[64,4,64]{2,1,0:T(4,128)} %broadcast_multiply_fusion.ac_ref, f32[64,4,64]{2,1,0:T(4,128)} %broadcast_in_dim.75.ab_ref, f32[64,4,64]{2,1,0:T(4,128)} %broadcast_select_fusion.seed_ref, ...), custom_call_target="tpu_custom_call" | custom-call | tf_op jit(solution)/shard_map/pallas_call | solution.py:373
  77.3 6.3 %shard_map.94 = f32[384,8,128]{2,1,0:T(8,128)} custom-call(bf16[4,8,32,384]{3,2,1,0:T(8,128)(2,1)} %shard_map.93.syn_ref, f32[8,128,384]{2,1,0:T(8,128)} %get-tuple-element.12.ac_ref, bf16[128,128]{1,0:T(8,128)(2,1)} %get-tuple-element.15.table_ref, bf16[384,384]{1,0:T(8,128)(2,1)} %mix_ref.1), custom_call_target="tpu_custom_call" | custom-call | tf_op jit(solution)/shard_map/pallas_call | solution.py:394
  (12 shorter events, 0.2 us)
Async XLA Ops:
  0.0 22.8 %copy-start = (f32[384]{0:T(512)S(1)}, f32[384]{0:T(512)}, u32[]{:S(2)}) copy-start(f32[384]{0:T(512)} %param.15) | copy-start | bytes 4612

commit v2 on v1

v2 whole, which is shorter than its diff:
```python
import functools
import math

import jax
import jax.numpy as jnp
from jax import lax
from jax.experimental import pallas as pl
from jax.experimental.pallas import tpu as pltpu
from jax.sharding import PartitionSpec as P

M_DEV = 8
HALO = 2
PAD = 16
LANES = 128
MESH = pl.DeviceIdType.MESH
VM = pl.BlockSpec(memory_space=pltpu.VMEM)
SM = pl.BlockSpec(memory_space=pltpu.SMEM)


def order_tables(forward_ref, inverse_ref, lon, nlon):
    width, all_q = inverse_ref.shape

    def wave(shape, q_axis):
        q = lax.broadcasted_iota(jnp.int32, shape, q_axis)
        j = lax.broadcasted_iota(jnp.int32, shape, 1 - q_axis) + lon * width
        turns = (j * (q >> 1) + (q & 1) * (nlon // 4)).astype(jnp.float32)
        turns = turns - nlon * jnp.floor(turns * (1.0 / nlon))
        return q, jnp.cos(turns * (2.0 * math.pi / nlon))

    q, cells = wave((all_q, width), 0)
    forward_ref[...] = (cells * (2.0 * math.pi / nlon)).astype(forward_ref.dtype)
    q, cells = wave((width, all_q), 1)
    inverse_ref[...] = (cells * jnp.where(q < 2, 1.0, 2.0)).astype(inverse_ref.dtype)


def legendre_table(table_ref, start_ref, first_q, modes):
    degrees, count, nlat = table_ref.shape
    shape = (count, nlat)

    def order_of(dims):
        q = lax.broadcasted_iota(jnp.int32, dims, 0) + first_q
        return (q >> 1).astype(jnp.float32)

    order = order_of(shape)
    colatitude = (
        (lax.broadcasted_iota(jnp.int32, shape, 1).astype(jnp.float32) + 0.5) * math.pi / nlat
    )
    cosine, sine = jnp.cos(colatitude), jnp.sin(colatitude)
    counters = lax.broadcasted_iota(jnp.int32, (count, modes), 1).astype(jnp.float32) + 1.0
    logs = jnp.log((2.0 * counters - 1.0) / (2.0 * counters))
    logs = jnp.where(counters <= order_of((count, modes)), logs, 0.0)
    log_product = jnp.sum(logs, axis=1, keepdims=True)
    log_seed = 0.5 * (
        jnp.log((2.0 * order + 1.0) / (4.0 * math.pi)) + log_product
    ) + order * jnp.log(sine)
    rescale = jnp.clip(-log_seed, 0.0, 80.0)
    seed = jnp.exp(log_seed + rescale)
    undo = jnp.exp(-rescale)
    square = order * order
    start_ref[...] = jnp.zeros(start_ref.shape, jnp.float32)

    def advance(degree, pair):
        previous, older = pair
        ell = degree.astype(jnp.float32)
        a = jnp.sqrt(
            jnp.maximum(4.0 * ell * ell - 1.0, 1.0) / jnp.maximum(ell * ell - square, 1.0)
        )
        below = (ell - 1.0) * (ell - 1.0)
        b = jnp.sqrt(jnp.maximum(below - square, 0.0) / jnp.maximum(4.0 * below - 1.0, 1.0))
        current = jnp.where(
            order == ell, seed, jnp.where(ell > order, a * (cosine * previous - b * older), 0.0)
        )
        table_ref[degree] = current * undo
        return (current, previous)

    lax.fori_loop(0, degrees, advance, (start_ref[0], start_ref[1]), unroll=4)


def field_kernel(
    lat_n, lon_n, modes,
    dlat_ref, dlon_ref, basis_ref, quad_ref, x_ref, w_ref, gain_ref, filt_ref,
    out_ref, ac_ref, inverse_ref,
    xp_ref, y_ref, forward, fp_ref, recv_a, send_b, recv_b, red, snd2, recv2,
    legendre, start, back, snd3,
    halo_s, halo_r, sa, ra, sb, rb, s2, r2, s3, r3, sx, rx, sp, rp, sf, rf,
):
    rows, width, chans = ac_ref.shape
    basis_count = w_ref.shape[0]
    taps = dlat_ref.shape[1]
    slabs = chans // LANES
    tall = xp_ref.shape[1]
    all_q = forward.shape[0]
    half = all_q // 2
    chips = lon_n // 2
    group = all_q // lon_n
    count = group // lat_n
    nlat, nlon = lat_n * rows, lon_n * width
    wire = snd2.dtype
    lat, lon = lax.axis_index("lat"), lax.axis_index("lon")
    up, down = lax.rem(lat + lat_n - 1, lat_n), lax.rem(lat + 1, lat_n)
    left, right = lax.rem(lon + lon_n - 1, lon_n), lax.rem(lon + 1, lon_n)
    chip, core = lon // 2, lax.rem(lon, 2)
    mate = chip * 2 + 1 - core

    def remote(source, target, send, recv, peer):
        return pltpu.make_async_remote_copy(
            src_ref=source, dst_ref=target, send_sem=send, recv_sem=recv,
            device_id=peer, device_id_type=MESH,
        )

    barrier = pltpu.get_barrier_semaphore()
    peers = [(lax.rem(lat + off, lat_n), lon) for off in range(1, lat_n)]
    peers += [(lat, lax.rem(lon + off, lon_n)) for off in range(1, lon_n)]
    peers += [(a, b) for a in (up, down) for b in (left, right)]
    for peer in peers:
        pl.semaphore_signal(barrier, inc=1, device_id=peer, device_id_type=MESH)

    def turn(row):
        cells = x_ref[:, row, :].T
        ac_ref[row] = cells
        xp_ref[row + HALO, PAD : PAD + width, :] = cells.astype(jnp.bfloat16)

    row_spans = {-1: (HALO, rows + HALO, HALO), 0: (HALO, HALO, rows), 1: (rows, 0, HALO)}
    col_spans = {-1: (PAD, PAD + width, PAD), 0: (PAD, PAD, width), 1: (width, 0, PAD)}

    def halo(dv, dh):
        peer = ({-1: up, 0: lat, 1: down}[dv], {-1: left, 0: lon, 1: right}[dh])
        rs, rd, rn = row_spans[dv]
        cs, cd, cn = col_spans[dh]
        index = (dv + 1) * 3 + dh + 1
        return remote(
            xp_ref.at[rs : rs + rn, cs : cs + cn, :],
            xp_ref.at[rd : rd + rn, cd : cd + cn, :],
            halo_s.at[index], halo_r.at[index], peer,
        )

    for row in list(range(HALO)) + list(range(rows - HALO, rows)):
        turn(row)
    pl.semaphore_wait(barrier, len(peers))
    across = [halo(dv, dh) for dv in (-1, 1) for dh in (0, -1, 1)]
    for copy in across:
        copy.start()
    for row in range(HALO, rows - HALO):
        turn(row)
    beside = [halo(0, dh) for dh in (-1, 1)]
    for copy in beside:
        copy.start()

    order_tables(forward, inverse_ref, lon, nlon)
    place = core * chips + chip
    legendre_table(legendre, start, place * group + lat * count, modes)
    for copy in beside:
        copy.wait()

    def mix(row):
        cells = xp_ref[row]
        for b in range(basis_count):
            mixed = jnp.dot(cells, w_ref[b], preferred_element_type=jnp.float32)
            for c in range(slabs):
                y_ref[b // 2, row, c, pl.ds(b % 2, tall, stride=2), :] = mixed[
                    :, c * LANES : (c + 1) * LANES
                ]

    step = 32

    def to_mate(row):
        return remote(
            fp_ref.at[row, 1 - core], recv_a.at[row], sa.at[row], ra.at[row], (lat, mate)
        )

    def to_chip(row, off):
        peer = lax.rem(chip + off, chips)
        return remote(
            send_b.at[row, peer], recv_b.at[off - 1, row],
            sb.at[row, off - 1], rb.at[row, off - 1], (lat, peer * 2 + core),
        )

    def conv(row):
        @pl.loop(0, width // step)
        def _(part):
            base = pl.multiple_of(part * step, step)
            totals = [
                ac_ref[row, pl.ds(base, step), c * LANES : (c + 1) * LANES] for c in range(slabs)
            ]
            for k in range(taps):
                basis = basis_ref[row, k]
                source = row + dlat_ref[row, k]
                globally = source + lat * rows
                inside = jnp.logical_and(globally >= 0, globally < nlat)
                scale = jnp.where(inside, quad_ref[row, k], 0.0)
                begin = 2 * (base + dlon_ref[row, k] + PAD) + (basis & 1)
                for c in range(slabs):
                    totals[c] = totals[c] + scale * y_ref[
                        basis >> 1, source + HALO, c, pl.ds(begin, step, stride=2), :
                    ]
            for c in range(slabs):
                ac_ref[row, pl.ds(base, step), c * LANES : (c + 1) * LANES] = totals[c]

        cells = ac_ref[row]
        mean = jnp.mean(cells * cells, axis=1, keepdims=True)
        normed = cells * lax.rsqrt(mean + 1e-06) * gain_ref[...]
        fp_ref[row] = jnp.dot(
            forward[...], normed.astype(jnp.bfloat16), preferred_element_type=jnp.float32
        ).astype(jnp.bfloat16).reshape(2, half, chans)
        to_mate(row).start()

    def pair(row):
        to_mate(row).wait()
        total = fp_ref[row, core].astype(jnp.float32) + recv_a[row].astype(jnp.float32)
        send_b[row] = total.astype(jnp.bfloat16).reshape(chips, group, chans)
        for off in range(1, chips):
            to_chip(row, off).start()

    def edge(index):
        return jnp.where(index < HALO, index, rows - 2 * HALO + index)

    @pl.loop(HALO, rows + HALO)
    def _(row):
        mix(row)

    @pl.loop(HALO, rows - HALO)
    def _(row):
        conv(row)

    for copy in across:
        copy.wait()

    @pl.loop(0, 2 * HALO)
    def _(index):
        mix(jnp.where(index < HALO, index, rows + index))

    @pl.loop(HALO, rows - HALO)
    def _(row):
        pair(row)

    @pl.loop(0, 2 * HALO)
    def _(index):
        conv(edge(index))

    @pl.loop(0, 2 * HALO)
    def _(index):
        pair(edge(index))

    for row in list(range(HALO, rows - HALO)) + list(range(HALO)) + list(range(rows - HALO, rows)):
        total = send_b[row, chip].astype(jnp.float32)
        for off in range(1, chips):
            to_chip(row, off).wait()
            total = total + recv_b[off - 1, row].astype(jnp.float32)
        red[:, row, :] = total
    for d in range(lat_n):
        snd2[d] = red[d * count : (d + 1) * count].reshape(count * rows, chans).astype(wire)

    second = []
    for off in range(1, lat_n):
        peer = lax.rem(lat + off, lat_n)
        copy = remote(
            snd2.at[peer], recv2.at[lat], s2.at[off - 1], r2.at[off - 1], (peer, lon)
        )
        copy.start()
        second.append(copy)
    recv2[lat] = snd2[lat]
    quad_weight = (math.pi / nlat) * jnp.sin(
        (lax.broadcasted_iota(jnp.int32, (1, nlat), 1).astype(jnp.float32) + 0.5) * math.pi / nlat
    )
    tables = [legendre[:, t, :] for t in range(count)]
    for copy in second:
        copy.wait()

    for t in range(count):
        cells = recv2[:, t * rows : (t + 1) * rows, :].astype(jnp.float32)
        cells = cells.reshape(lat_n * rows, chans).astype(jnp.bfloat16)
        analysis = (tables[t] * quad_weight).astype(jnp.bfloat16)
        spectra = jnp.dot(analysis, cells, preferred_element_type=jnp.float32)
        filtered = (spectra * filt_ref[...]).astype(jnp.bfloat16)
        result = jnp.dot(
            tables[t].T.astype(jnp.bfloat16), filtered, preferred_element_type=jnp.float32
        )
        back[:, t * rows : (t + 1) * rows, :] = result.reshape(lat_n, rows, chans)
    for d in range(lat_n):
        snd3[d] = back[d].astype(wire)

    third = []
    for off in range(1, lat_n):
        peer = lax.rem(lat + off, lat_n)
        copy = remote(
            snd3.at[peer], out_ref.at[place, lat], s3.at[off - 1], r3.at[off - 1], (peer, lon)
        )
        copy.start()
        third.append(copy)
    out_ref[place, lat] = snd3[lat]

    last = []

    def spread(slot):
        source = lax.rem(lat + lat_n - slot, lat_n)
        block = out_ref.at[place, source]
        hops = []
        for off in range(1, chips):
            peer = lax.rem(chip + off, chips)
            hops.append(
                remote(
                    block, block, sx.at[slot, off - 1], rx.at[slot, off - 1],
                    (lat, peer * 2 + core),
                )
            )
            hops[-1].start()
        last.append(remote(block, block, sp.at[slot], rp.at[slot], (lat, mate)))
        last[-1].start()
        return hops

    def forward_on(slot, hops):
        source = lax.rem(lat + lat_n - slot, lat_n)
        for off in range(1, chips):
            hops[off - 1].wait()
            origin = core * chips + lax.rem(chip + chips - off, chips)
            block = out_ref.at[origin, source]
            last.append(
                remote(block, block, sf.at[slot, off - 1], rf.at[slot, off - 1], (lat, mate))
            )
            last[-1].start()

    hops = {}
    for slot in range(lat_n):
        if slot:
            third[slot - 1].wait()
        hops[slot] = spread(slot)
        if slot >= 3:
            forward_on(slot - 3, hops[slot - 3])
    for slot in range(max(lat_n - 3, 0), lat_n):
        forward_on(slot, hops[slot])
    for copy in last:
        copy.wait()


def output_kernel(syn_ref, ac_ref, table_ref, mix_ref, o_ref, wide):
    rows, width, chans = ac_ref.shape
    all_q = table_ref.shape[1]
    wide[...] = syn_ref[...].astype(jnp.float32).reshape(all_q, rows, chans)
    for row in range(rows):
        waves = wide[:, row, :].astype(jnp.bfloat16)
        field = jnp.dot(table_ref[...], waves, preferred_element_type=jnp.float32)
        active = jax.nn.gelu(field, approximate=True).astype(jnp.bfloat16)
        total = ac_ref[row] + jnp.dot(active, mix_ref[...], preferred_element_type=jnp.float32)
        o_ref[:, row, :] = total.T


def per_device(
    grid_field,
    disco_dlat,
    disco_dlon,
    disco_basis,
    disco_quad,
    disco_weight,
    norm_gain,
    spectral_filter,
    mix_weight,
):
    lat_n = lax.axis_size("lat")
    lon_n = lax.axis_size("lon")
    chans, rows, width = grid_field.shape
    nlat, nlon = rows * lat_n, width * lon_n
    modes = M_DEV * lat_n
    all_q = 2 * modes
    degrees = spectral_filter.shape[1]
    group = all_q // lon_n
    count = group // lat_n
    basis_count = disco_weight.shape[0]
    f32, bf16 = jnp.float32, jnp.bfloat16

    wire = bf16 if (count * rows) % 16 == 0 else f32
    block = (lat_n, count * rows, chans)
    chips = lon_n // 2
    tall = width + 2 * PAD
    dma = pltpu.SemaphoreType.DMA
    vmem = pltpu.VMEM
    synthesis, after_conv, inverse = pl.pallas_call(
        functools.partial(field_kernel, lat_n, lon_n, modes),
        out_shape=(
            jax.ShapeDtypeStruct((lon_n,) + block, wire),
            jax.ShapeDtypeStruct((rows, width, chans), f32),
            jax.ShapeDtypeStruct((width, all_q), bf16),
        ),
        in_specs=[SM] * 4 + [VM] * 4,
        out_specs=(VM, VM, VM),
        scratch_shapes=[
            vmem((rows + 2 * HALO, tall, chans), bf16),
            vmem(
                ((basis_count + 1) // 2, rows + 2 * HALO, chans // LANES, 2 * tall, LANES), f32
            ),
            vmem((all_q, width), bf16),
            vmem((rows, 2, all_q // 2, chans), bf16),
            vmem((rows, all_q // 2, chans), bf16),
            vmem((rows, chips, group, chans), bf16),
            vmem((chips - 1, rows, group, chans), bf16),
            vmem((group, rows, chans), f32),
            vmem(block, wire),
            vmem(block, wire),
            vmem((degrees, count, nlat), f32),
            vmem((2, count, nlat), f32),
            vmem(block, f32),
            vmem(block, wire),
            dma((9,)), dma((9,)),
            dma((rows,)), dma((rows,)),
            dma((rows, chips - 1)), dma((rows, chips - 1)),
            dma((lat_n - 1,)), dma((lat_n - 1,)),
            dma((lat_n - 1,)), dma((lat_n - 1,)),
            dma((lat_n, chips - 1)), dma((lat_n, chips - 1)),
            dma((lat_n,)), dma((lat_n,)),
            dma((lat_n, chips - 1)), dma((lat_n, chips - 1)),
        ],
        compiler_params=pltpu.CompilerParams(collective_id=0, has_side_effects=True),
    )(
        disco_dlat, disco_dlon, disco_basis, disco_quad,
        grid_field, disco_weight, norm_gain[None, :], spectral_filter.T,
    )

    return pl.pallas_call(
        output_kernel,
        out_shape=jax.ShapeDtypeStruct((chans, rows, width), f32),
        in_specs=[VM] * 4,
        out_specs=VM,
        scratch_shapes=[pltpu.VMEM((all_q, rows, chans), f32)],
    )(synthesis, after_conv, inverse, mix_weight)


def solution(mesh):
    placed = (
        P(None, "lat", "lon"),
        P("lat", None),
        P("lat", None),
        P("lat", None),
        P("lat", None),
        P(),
        P(),
        P(),
        P(),
    )
    return jax.shard_map(
        per_device, mesh=mesh, in_specs=placed, out_specs=P(None, "lat", "lon"), check_vma=False
    )
```

time: 83.8 us -> 58.3 us (0.70)
  Pallas kernels: 74.9 us -> 56.9 us
  other arithmetic: 7.2 us -> 0 us
    pallas_call x3 -> x1, Pallas kernels: 68.7 us -> 50.6 us  [per_device(): pl.pallas_call(functools.partial(field_kernel, lat_n, lon_n, modes), out_...]
    select_n x4 -> x0, other arithmetic: 2.1 us -> none  [the longest x1 1.31 us: per_device(): quad = jnp.where((globally >= 0) & (globally < nlat), disco_quad, 0.0)]
    mul x4 -> x0, other arithmetic: 1.55 us -> none  [the longest x1 0.8 us: per_device(): a_cos = a * cosine[None, None, :]]
    add x3 -> x0, other arithmetic: 1.34 us -> none  [the longest x1 1.33 us: per_device(): source + HALO]
    convert_element_type x2 -> x0, other arithmetic: 1.19 us -> none  [the longest x1 1.18 us: per_device(): inverse = (wave * jnp.where(q_pos < 2, 1.0, 2.0)[None, :]).astype(bf16)]
where the time goes in v2:
time: 58.3 us; the launch traced here: 58.1 us
  Pallas kernels  56.9 us (98%)
  local copies, waits for them, and re-layouts  1.24 us (2%)
    pallas_call x1, Pallas kernels, per_device(): pl.pallas_call(functools.partial(field_kernel, lat_n, lon_n, modes), out_...  50.6 us
    pallas_call x1, Pallas kernels, per_device(): pl.pallas_call(output_kernel, out_shape=jax.ShapeDtypeStruct((chans, rows...  6.28 us
    broadcast_in_dim x1, local copies, waits for them, and re-layouts, per_device(): norm_gain[None, :]  1.24 us

profile of v2, /device:TPU:0, one launch (start us, length us, event | category | flops | bytes accessed | tf_op | source)
XLA Modules:
  0.0 58.1 jit_solution(15742003297586594618)
XLA Ops:
  0.0 1.2 %broadcast_in_dim.3.gain_ref = f32[1,384]{1,0:T(1,128)} reshape(f32[384]{0:T(512)} %param.15) | data formatting | bytes 3072 | tf_op jit(solution)/shard_map/broadcast_in_dim | solution.py:414
  1.2 50.6 %shard_map.91 = (bf16[4,8,32,384]{3,2,1,0:T(8,128)(2,1)}, f32[8,128,384]{2,1,0:T(8,128)}, bf16[128,128]{1,0:T(8,128)(2,1)}) custom-call(s32[8,16]{1,0:T(8,128)} %dlat_ref.1, s32[8,16]{1,0:T(8,128)} %dlon_ref.1, s32[8,16]{1,0:T(8,128)} %basis_ref.1, f32[8,16]{1,0:T(8,128)} %quad_ref.1, f32[384,8,128]{2,1,0:T(8,128)} %x_ref.1, bf16[4,384,384]{2,1,0:T(8,128)(2,1)} %w_ref.1, ...), custom_call_target="tpu_custom_call" | custom-call | tf_op jit(solution)/shard_map/pallas_call | solution.py:376
  51.8 6.3 %shard_map.92 = f32[384,8,128]{2,1,0:T(8,128)} custom-call(bf16[4,8,32,384]{3,2,1,0:T(8,128)(2,1)} %get-tuple-element.8.syn_ref, f32[8,128,384]{2,1,0:T(8,128)} %get-tuple-element.9.ac_ref, bf16[128,128]{1,0:T(8,128)(2,1)} %get-tuple-element.10.table_ref, bf16[384,384]{1,0:T(8,128)(2,1)} %mix_ref.1), custom_call_target="tpu_custom_call" | custom-call | tf_op jit(solution)/shard_map/pallas_call | solution.py:417

commit v3 on v2

--- a/solution.py
+++ b/solution.py
@@ -15,6 +15,7 @@
 MESH = pl.DeviceIdType.MESH
 VM = pl.BlockSpec(memory_space=pltpu.VMEM)
 SM = pl.BlockSpec(memory_space=pltpu.SMEM)
+HB = pl.BlockSpec(memory_space=pl.ANY)
 
 
 def order_tables(forward_ref, inverse_ref, lon, nlon):
@@ -78,8 +79,9 @@
 
 def field_kernel(
     lat_n, lon_n, modes,
-    dlat_ref, dlon_ref, basis_ref, quad_ref, x_ref, w_ref, gain_ref, filt_ref,
-    out_ref, ac_ref, inverse_ref,
+    dlat_ref, dlon_ref, basis_ref, quad_ref, x_hbm, w_hbm, gain_ref, filt_ref,
+    out_ref, ac_hbm, inverse_ref,
+    x_ref, w_ref, ac_ref, load_x, load_w, store_ac,
     xp_ref, y_ref, forward, fp_ref, recv_a, send_b, recv_b, red, snd2, recv2,
     legendre, start, back, snd3,
     halo_s, halo_r, sa, ra, sb, rb, s2, r2, s3, r3, sx, rx, sp, rp, sf, rf,
@@ -115,10 +117,19 @@
     for peer in peers:
         pl.semaphore_signal(barrier, inc=1, device_id=peer, device_id_type=MESH)
 
-    def turn(row):
-        cells = x_ref[:, row, :].T
-        ac_ref[row] = cells
-        xp_ref[row + HALO, PAD : PAD + width, :] = cells.astype(jnp.bfloat16)
+    loads = []
+    for c in range(slabs):
+        part = slice(c * LANES, (c + 1) * LANES)
+        loads.append(pltpu.make_async_copy(x_hbm.at[part], x_ref.at[part], load_x.at[c]))
+        loads[-1].start()
+    weights = pltpu.make_async_copy(w_hbm, w_ref, load_w)
+    weights.start()
+
+    def turn(row, c):
+        part = slice(c * LANES, (c + 1) * LANES)
+        cells = x_ref[part, row, :].T
+        ac_ref[row, :, part] = cells
+        xp_ref[row + HALO, PAD : PAD + width, part] = cells.astype(jnp.bfloat16)
 
     row_spans = {-1: (HALO, rows + HALO, HALO), 0: (HALO, HALO, rows), 1: (rows, 0, HALO)}
     col_spans = {-1: (PAD, PAD + width, PAD), 0: (PAD, PAD, width), 1: (width, 0, PAD)}
@@ -134,14 +145,17 @@
             halo_s.at[index], halo_r.at[index], peer,
         )
 
-    for row in list(range(HALO)) + list(range(rows - HALO, rows)):
-        turn(row)
+    for c in range(slabs):
+        loads[c].wait()
+        for row in list(range(HALO)) + list(range(rows - HALO, rows)):
+            turn(row, c)
     pl.semaphore_wait(barrier, len(peers))
     across = [halo(dv, dh) for dv in (-1, 1) for dh in (0, -1, 1)]
     for copy in across:
         copy.start()
     for row in range(HALO, rows - HALO):
-        turn(row)
+        for c in range(slabs):
+            turn(row, c)
     beside = [halo(0, dh) for dh in (-1, 1)]
     for copy in beside:
         copy.start()
@@ -149,6 +163,7 @@
     order_tables(forward, inverse_ref, lon, nlon)
     place = core * chips + chip
     legendre_table(legendre, start, place * group + lat * count, modes)
+    weights.wait()
     for copy in beside:
         copy.wait()
 
@@ -174,6 +189,9 @@
             send_b.at[row, peer], recv_b.at[off - 1, row],
             sb.at[row, off - 1], rb.at[row, off - 1], (lat, peer * 2 + core),
         )
+
+    def put(row):
+        return pltpu.make_async_copy(ac_ref.at[row], ac_hbm.at[row], store_ac.at[row])
 
     def conv(row):
         @pl.loop(0, width // step)
@@ -196,9 +214,10 @@
             for c in range(slabs):
                 ac_ref[row, pl.ds(base, step), c * LANES : (c + 1) * LANES] = totals[c]
 
+        put(row).start()
         cells = ac_ref[row]
         mean = jnp.mean(cells * cells, axis=1, keepdims=True)
-        normed = cells * lax.rsqrt(mean + 1e-06) * gain_ref[...]
+        normed = cells * lax.rsqrt(mean + 1e-06) * gain_ref[...][None, :]
         fp_ref[row] = jnp.dot(
             forward[...], normed.astype(jnp.bfloat16), preferred_element_type=jnp.float32
         ).astype(jnp.bfloat16).reshape(2, half, chans)
@@ -222,16 +241,16 @@
     def _(row):
         conv(row)
 
+    @pl.loop(HALO, rows - HALO)
+    def _(row):
+        pair(row)
+
     for copy in across:
         copy.wait()
 
     @pl.loop(0, 2 * HALO)
     def _(index):
         mix(jnp.where(index < HALO, index, rows + index))
-
-    @pl.loop(HALO, rows - HALO)
-    def _(row):
-        pair(row)
 
     @pl.loop(0, 2 * HALO)
     def _(index):
@@ -330,17 +349,27 @@
         forward_on(slot, hops[slot])
     for copy in last:
         copy.wait()
-
-
-def output_kernel(syn_ref, ac_ref, table_ref, mix_ref, o_ref, wide):
-    rows, width, chans = ac_ref.shape
+    for row in range(rows):
+        put(row).wait()
+
+
+def output_kernel(syn_ref, ac_ref, table_ref, mix_ref, o_ref, wide, active):
+    rows, width, _ = ac_ref.shape
     all_q = table_ref.shape[1]
-    wide[...] = syn_ref[...].astype(jnp.float32).reshape(all_q, rows, chans)
+    chans = mix_ref.shape[0]
+
+    @pl.when(pl.program_id(0) == 0)
+    def _():
+        wide[...] = syn_ref[...].astype(jnp.float32).reshape(all_q, rows, chans)
+        for row in range(rows):
+            waves = wide[:, row, :].astype(jnp.bfloat16)
+            field = jnp.dot(table_ref[...], waves, preferred_element_type=jnp.float32)
+            active[row] = jax.nn.gelu(field, approximate=True).astype(jnp.bfloat16)
+
     for row in range(rows):
-        waves = wide[:, row, :].astype(jnp.bfloat16)
-        field = jnp.dot(table_ref[...], waves, preferred_element_type=jnp.float32)
-        active = jax.nn.gelu(field, approximate=True).astype(jnp.bfloat16)
-        total = ac_ref[row] + jnp.dot(active, mix_ref[...], preferred_element_type=jnp.float32)
+        total = ac_ref[row] + jnp.dot(
+            active[row], mix_ref[...], preferred_element_type=jnp.float32
+        )
         o_ref[:, row, :] = total.T
 
 
@@ -380,9 +409,13 @@
             jax.ShapeDtypeStruct((rows, width, chans), f32),
             jax.ShapeDtypeStruct((width, all_q), bf16),
         ),
-        in_specs=[SM] * 4 + [VM] * 4,
-        out_specs=(VM, VM, VM),
+        in_specs=[SM] * 4 + [HB, HB, VM, VM],
+        out_specs=(VM, HB, VM),
         scratch_shapes=[
+            vmem((chans, rows, width), f32),
+            vmem(disco_weight.shape, bf16),
+            vmem((rows, width, chans), f32),
+            dma((chans // LANES,)), dma, dma((rows,)),
             vmem((rows + 2 * HALO, tall, chans), bf16),
             vmem(
                 ((basis_count + 1) // 2, rows + 2 * HALO, chans // LANES, 2 * tall, LANES), f32
@@ -411,15 +444,22 @@
         compiler_params=pltpu.CompilerParams(collective_id=0, has_side_effects=True),
     )(
         disco_dlat, disco_dlon, disco_basis, disco_quad,
-        grid_field, disco_weight, norm_gain[None, :], spectral_filter.T,
+        grid_field, disco_weight, norm_gain, spectral_filter.T,
     )
 
+    whole = lambda shape: pl.BlockSpec(shape, lambda o: (0,) * len(shape))
     return pl.pallas_call(
         output_kernel,
+        grid=(chans // LANES,),
         out_shape=jax.ShapeDtypeStruct((chans, rows, width), f32),
-        in_specs=[VM] * 4,
-        out_specs=VM,
-        scratch_shapes=[pltpu.VMEM((all_q, rows, chans), f32)],
+        in_specs=[
+            whole(synthesis.shape),
+            pl.BlockSpec((rows, width, LANES), lambda o: (0, 0, o)),
+            whole(inverse.shape),
+            pl.BlockSpec((chans, LANES), lambda o: (0, o)),
+        ],
+        out_specs=pl.BlockSpec((LANES, rows, width), lambda o: (o, 0, 0)),
+        scratch_shapes=[vmem((all_q, rows, chans), f32), vmem((rows, width, chans), bf16)],
     )(synthesis, after_conv, inverse, mix_weight)
 
 

time: 58.3 us -> 57.2 us (0.981)
  local copies, waits for them, and re-layouts: 1.24 us -> 0 us
    broadcast_in_dim x1 -> x0, local copies, waits for them, and re-layouts: 1.24 us -> none  [per_device(): norm_gain[None, :]]
where the time goes in v3:
time: 57.2 us; the launch traced here: 57 us
  Pallas kernels  57 us (100%)
    pallas_call x1, Pallas kernels, per_device(): pl.pallas_call(functools.partial(field_kernel, lat_n, lon_n, modes), out_...  50.2 us
    pallas_call x1, Pallas kernels, per_device(): pl.pallas_call(output_kernel, grid=(chans // LANES,), out_shape=jax.Shape...  6.75 us

profile of v3, /device:TPU:0, one launch (start us, length us, event | category | flops | bytes accessed | tf_op | source)
XLA Modules:
  0.0 57.0 jit_solution(4271296191610637343)
XLA Ops:
  0.0 50.2 %shard_map.91 = (bf16[4,8,32,384]{3,2,1,0:T(8,128)(2,1)}, f32[8,128,384]{2,1,0:T(8,128)}, bf16[128,128]{1,0:T(8,128)(2,1)}) custom-call(s32[8,16]{1,0:T(8,128)} %dlat_ref.1, s32[8,16]{1,0:T(8,128)} %dlon_ref.1, s32[8,16]{1,0:T(8,128)} %basis_ref.1, f32[8,16]{1,0:T(8,128)} %quad_ref.1, f32[384,8,128]{2,1,0:T(8,128)} %x_hbm.1, bf16[4,384,384]{2,1,0:T(8,128)(2,1)} %w_hbm.1, ...), custom_call_target="tpu_custom_call" | custom-call | tf_op jit(solution)/shard_map/pallas_call | solution.py:405
  50.2 6.7 %shard_map.92 = f32[384,8,128]{2,1,0:T(8,128)} custom-call(bf16[4,8,32,384]{3,2,1,0:T(8,128)(2,1)} %get-tuple-element.8.syn_ref, f32[8,128,384]{2,1,0:T(8,128)} %get-tuple-element.9.ac_ref, bf16[128,128]{1,0:T(8,128)(2,1)} %get-tuple-element.10.table_ref, bf16[384,384]{1,0:T(8,128)(2,1)} %mix_ref.1), custom_call_target="tpu_custom_call" | custom-call | tf_op jit(solution)/shard_map/pallas_call | solution.py:451

commit v4 on v3

--- a/solution.py
+++ b/solution.py
@@ -176,7 +176,7 @@
                     :, c * LANES : (c + 1) * LANES
                 ]
 
-    step = 32
+    step = 64
 
     def to_mate(row):
         return remote(
@@ -233,7 +233,7 @@
     def edge(index):
         return jnp.where(index < HALO, index, rows - 2 * HALO + index)
 
-    @pl.loop(HALO, rows + HALO)
+    @pl.loop(HALO, rows + HALO, unroll=2)
     def _(row):
         mix(row)
 
@@ -248,7 +248,7 @@
     for copy in across:
         copy.wait()
 
-    @pl.loop(0, 2 * HALO)
+    @pl.loop(0, 2 * HALO, unroll=2)
     def _(index):
         mix(jnp.where(index < HALO, index, rows + index))
 
@@ -353,23 +353,15 @@
         put(row).wait()
 
 
-def output_kernel(syn_ref, ac_ref, table_ref, mix_ref, o_ref, wide, active):
-    rows, width, _ = ac_ref.shape
+def output_kernel(syn_ref, ac_ref, table_ref, mix_ref, o_ref, wide):
+    rows, width, chans = ac_ref.shape
     all_q = table_ref.shape[1]
-    chans = mix_ref.shape[0]
-
-    @pl.when(pl.program_id(0) == 0)
-    def _():
-        wide[...] = syn_ref[...].astype(jnp.float32).reshape(all_q, rows, chans)
-        for row in range(rows):
-            waves = wide[:, row, :].astype(jnp.bfloat16)
-            field = jnp.dot(table_ref[...], waves, preferred_element_type=jnp.float32)
-            active[row] = jax.nn.gelu(field, approximate=True).astype(jnp.bfloat16)
-
+    wide[...] = syn_ref[...].astype(jnp.float32).reshape(all_q, rows, chans)
     for row in range(rows):
-        total = ac_ref[row] + jnp.dot(
-            active[row], mix_ref[...], preferred_element_type=jnp.float32
-        )
+        waves = wide[:, row, :].astype(jnp.bfloat16)
+        field = jnp.dot(table_ref[...], waves, preferred_element_type=jnp.float32)
+        active = jax.nn.gelu(field, approximate=True).astype(jnp.bfloat16)
+        total = ac_ref[row] + jnp.dot(active, mix_ref[...], preferred_element_type=jnp.float32)
         o_ref[:, row, :] = total.T
 
 
@@ -447,19 +439,12 @@
         grid_field, disco_weight, norm_gain, spectral_filter.T,
     )
 
-    whole = lambda shape: pl.BlockSpec(shape, lambda o: (0,) * len(shape))
     return pl.pallas_call(
         output_kernel,
-        grid=(chans // LANES,),
         out_shape=jax.ShapeDtypeStruct((chans, rows, width), f32),
-        in_specs=[
-            whole(synthesis.shape),
-            pl.BlockSpec((rows, width, LANES), lambda o: (0, 0, o)),
-            whole(inverse.shape),
-            pl.BlockSpec((chans, LANES), lambda o: (0, o)),
-        ],
-        out_specs=pl.BlockSpec((LANES, rows, width), lambda o: (o, 0, 0)),
-        scratch_shapes=[vmem((all_q, rows, chans), f32), vmem((rows, width, chans), bf16)],
+        in_specs=[VM] * 4,
+        out_specs=VM,
+        scratch_shapes=[pltpu.VMEM((all_q, rows, chans), f32)],
     )(synthesis, after_conv, inverse, mix_weight)
 
 

time: 57.2 us -> 54.5 us (0.953)
  Pallas kernels: 57 us -> 54.3 us
    pallas_call x1, Pallas kernels: 50.2 us -> 48 us  [per_device(): pl.pallas_call(functools.partial(field_kernel, lat_n, lon_n, modes), out_...]
where the time goes in v4:
time: 54.5 us; the launch traced here: 54.3 us
  Pallas kernels  54.3 us (100%)
    pallas_call x1, Pallas kernels, per_device(): pl.pallas_call(functools.partial(field_kernel, lat_n, lon_n, modes), out_...  48 us
    pallas_call x1, Pallas kernels, per_device(): pl.pallas_call(output_kernel, out_shape=jax.ShapeDtypeStruct((chans, rows...  6.28 us

profile of v4, /device:TPU:0, one launch (start us, length us, event | category | flops | bytes accessed | tf_op | source)
XLA Modules:
  0.0 54.3 jit_solution(4334616485531665948)
XLA Ops:
  0.0 48.0 %shard_map.91 = (bf16[4,8,32,384]{3,2,1,0:T(8,128)(2,1)}, f32[8,128,384]{2,1,0:T(8,128)}, bf16[128,128]{1,0:T(8,128)(2,1)}) custom-call(s32[8,16]{1,0:T(8,128)} %dlat_ref.1, s32[8,16]{1,0:T(8,128)} %dlon_ref.1, s32[8,16]{1,0:T(8,128)} %basis_ref.1, f32[8,16]{1,0:T(8,128)} %quad_ref.1, f32[384,8,128]{2,1,0:T(8,128)} %x_hbm.1, bf16[4,384,384]{2,1,0:T(8,128)(2,1)} %w_hbm.1, ...), custom_call_target="tpu_custom_call" | custom-call | tf_op jit(solution)/shard_map/pallas_call | solution.py:397
  48.0 6.3 %shard_map.92 = f32[384,8,128]{2,1,0:T(8,128)} custom-call(bf16[4,8,32,384]{3,2,1,0:T(8,128)(2,1)} %get-tuple-element.8.syn_ref, f32[8,128,384]{2,1,0:T(8,128)} %get-tuple-element.9.ac_ref, bf16[128,128]{1,0:T(8,128)(2,1)} %get-tuple-element.10.table_ref, bf16[384,384]{1,0:T(8,128)(2,1)} %mix_ref.1), custom_call_target="tpu_custom_call" | custom-call | tf_op jit(solution)/shard_map/pallas_call | solution.py:442
